TPU v7x, 128 devices: a whole 4x4x4 slice. The times are simulated.
128 devices in a mesh: dp: 8 (over z, core), ctx: 16 (over x, y).
Axes of the slice: x: 4, y: 4, z: 4, core: 2. Of those that a mesh axis runs over, the one named last changes fastest.
Arguments:
- tokens: bfloat16 [32768, 2048], P(('dp', 'ctx')), parts along dimension 0, may hold values from -80 to 80
- qkv_weight: bfloat16 [2048, 3072], P('ctx'), may hold values from -0.125 to 0.125
- out_weight: bfloat16 [1024, 2048], P('ctx'), may hold values from -0.1875 to 0.1875
- prior_state: float32 [64, 128, 128], P('dp'), parts along dimension 0, may hold values from -240 to 240
- expert_ids: int32 [32768, 4], P(('dp', 'ctx')), parts along dimension 0, may hold values from 0 to 15, all different within a row; in each aligned block of 256 rows (0 to 255, 256 to 511, ...) at most 96 rows name the same one
- gate_weights: float32 [32768, 4], P(('dp', 'ctx')), parts along dimension 0, may hold values from 0.1 to 1
- expert_in: bfloat16 [16, 2048, 2048], P('ctx'), may hold values from -0.125 to 0.125
- expert_out: bfloat16 [16, 1024, 2048], P('ctx'), may hold values from -0.1875 to 0.1875
Outputs:
- layer_out: bfloat16 [32768, 2048], P(('dp', 'ctx')), parts along dimension 0
There are 8 independent parts, one for each index of `dp`. A program takes and returns all parts, laid end to end along the dimension named above; an argument that names none is the same for every part. Nothing has to cross between parts.
Inputs may be any that keep to these rules, and one draw needn't show every extreme that they name: `expert_ids`: within the 256 rows of one device no expert is named more than 96 times, and in some device's rows some expert is named exactly 96 times.
All inputs are finite; a program needn't handle non-finite values.
Results may differ from a plain program's by a relative error of at most 0.006.
Values may be sent and summed in bfloat16 or wider, within the bound.
No kernel may reach another device: no remote copies, remote signals or barrier semaphores. Data moves between devices by JAX's collectives and lax.ppermute only.
A program may use at most 128 MiB of HBM per device.

v0:
```python
import jax
import jax.numpy as jnp
from jax import lax
from jax.sharding import PartitionSpec as P

HEADS = 8
HD = 128
FF = 1024
EPSILON = 1e-05


def prefix(x, axis, combine, identity):
    length, index = (lax.axis_size(axis), lax.axis_index(axis))
    everything = lax.all_gather(x.astype(jnp.bfloat16), axis)
    start = jnp.broadcast_to(jnp.asarray(identity, x.dtype), x.shape)

    def step(k, before):
        reached = k < index
        new = combine(before, everything[k].astype(x.dtype))
        return jnp.where(reached, new, before)

    return lax.fori_loop(0, length, step, start)


def rms_rows(matrix):
    return matrix * lax.rsqrt(jnp.mean(matrix * matrix, axis=-1, keepdims=True) + EPSILON)


def combine_add(earlier, later):
    return earlier + later


def shards(
    tokens, qkv_weight, out_weight, prior_state, expert_ids, gate_weights, expert_in, expert_out
):
    tok_rows = tokens.shape[0]
    model_width = tokens.shape[1]
    width_heads = HEADS * HD
    groups = lax.axis_size("ctx")
    local_experts = expert_in.shape[0]
    experts = local_experts * groups
    top_count = expert_ids.shape[1]
    capacity = 3 * tok_rows * top_count // (2 * experts)
    normed = rms_rows(tokens.astype(jnp.float32)).astype(jnp.bfloat16)
    columns = normed
    projected = jnp.dot(
        columns,
        lax.all_gather(qkv_weight, "ctx", axis=0, tiled=True),
        preferred_element_type=jnp.float32,
    )
    queries = (
        jax.nn.silu(projected[:, :width_heads]).astype(jnp.bfloat16).reshape(tok_rows, HEADS, HD)
    )
    key_rows = (
        jax.nn.silu(projected[:, width_heads : 2 * width_heads])
        .astype(jnp.bfloat16)
        .reshape(tok_rows, HEADS, HD)
    )
    value_rows = projected[:, 2 * width_heads :].astype(jnp.bfloat16).reshape(tok_rows, HEADS, HD)
    local_state = jnp.einsum(
        "thd,the->hde", key_rows, value_rows, preferred_element_type=jnp.float32
    )
    earlier_sum = prefix(local_state, "ctx", combine_add, jnp.zeros_like(local_state))
    carried = prior_state + earlier_sum
    scores = jnp.einsum("thd,shd->hts", queries, key_rows, preferred_element_type=jnp.float32)
    causal = (
        jnp.arange(tok_rows, dtype=jnp.int32)[:, None]
        >= jnp.arange(tok_rows, dtype=jnp.int32)[None, :]
    )
    scores = jnp.where(causal[None], scores, jnp.float32(0.0)).astype(jnp.bfloat16)
    inside = jnp.einsum("hts,she->the", scores, value_rows, preferred_element_type=jnp.float32)
    from_state = jnp.einsum(
        "thd,hde->the", queries.astype(jnp.float32), carried, precision=lax.Precision.HIGHEST
    )
    head_normed = rms_rows(from_state + inside).astype(jnp.bfloat16).reshape(tok_rows, width_heads)
    columns = head_normed
    attended = jnp.dot(
        columns,
        lax.all_gather(out_weight, "ctx", axis=0, tiled=True),
        preferred_element_type=jnp.float32,
    )
    hidden = (tokens.astype(jnp.float32) + attended).astype(jnp.bfloat16)
    moe_in = rms_rows(hidden.astype(jnp.float32)).astype(jnp.bfloat16)
    flat_ids = expert_ids.reshape(-1)
    onehot = (flat_ids[:, None] == jnp.arange(experts, dtype=jnp.int32)[None, :]).astype(jnp.int32)
    before = jnp.cumsum(onehot, axis=0) - onehot
    slot_index = jnp.sum(before * onehot, axis=1)
    places = flat_ids * capacity + slot_index
    repeated = jnp.repeat(moe_in, top_count, axis=0)
    outgoing = jnp.zeros((experts * capacity, model_width), jnp.bfloat16).at[places].set(repeated)
    outgoing = outgoing.reshape(experts, capacity, model_width)
    arrived = lax.all_to_all(outgoing, "ctx", split_axis=0, concat_axis=0, tiled=True)
    slot_count = arrived.shape[1]
    grouped = arrived.reshape(groups, local_experts, slot_count, model_width)
    gate_up = jnp.einsum("nxid,xdf->nxif", grouped, expert_in, preferred_element_type=jnp.float32)
    middle = (jax.nn.silu(gate_up[..., :FF]) * gate_up[..., FF:]).astype(jnp.bfloat16)
    result = jnp.einsum(
        "nxif,xfd->nxid", middle, expert_out, preferred_element_type=jnp.float32
    ).astype(jnp.bfloat16)
    finished = result.reshape(groups * local_experts, slot_count, model_width)
    returned = lax.all_to_all(finished, "ctx", split_axis=0, concat_axis=0, tiled=True).reshape(
        experts * capacity, model_width
    )
    picked = returned[places].reshape(tok_rows, top_count, model_width).astype(jnp.float32)
    combined = jnp.sum(gate_weights[:, :, None] * picked, axis=1)
    return (hidden.astype(jnp.float32) + combined).astype(jnp.bfloat16)


def solution(mesh):
    return jax.shard_map(
        shards,
        mesh=mesh,
        in_specs=(
            P(("dp", "ctx"), None),
            P("ctx", None),
            P("ctx", None),
            P("dp", None, None),
            P(("dp", "ctx"), None),
            P(("dp", "ctx"), None),
            P("ctx", None, None),
            P("ctx", None, None),
        ),
        out_specs=P(("dp", "ctx"), None),
        check_vma=False,
    )
```

profile of v0, /device:TPU:28, one launch (start us, length us, event | category | flops | bytes accessed | tf_op | source)
XLA Modules:
  0.0 480.7 jit_solution(9268005951179839358)
XLA Ops:
  6.5 0.7 all-gather.5.cloned.1.call-update
  7.3 1.5 fusion.12
  8.8 91.1 %all-gather.5.cloned.1.call-done = bf16[2048,3072]{1,0:T(8,128)(2,1)} async-done(((bf16[128,3072]{1,0:T(8,128)(2,1)}), bf16[2048,3072]{1,0:T(8,128)(2,1)}) %all-gather.5.cloned.1.call-update) | async-done | bytes 12582928 | tf_op jit(solution)/shard_map/all_gather | solution.py:48
  99.9 6.8 %fusion.20 = f32[256,3072]{1,0:T(8,128)S(1)} fusion(bf16[2048,3072]{1,0:T(8,128)(2,1)} %all-gather.5.cloned.1.call-done, bf16[256,2048]{1,0:T(8,128)(2,1)} %param.10, f32[256]{0:T(256)S(1)} %add_rsqrt_fusion.2), kind=kOutput, calls=%fused_computation.31 | convolution fusion | flops 3222798336 | bytes 16778240 | tf_op jit(solution)/shard_map/dot_general | solution.py:46
  106.7 0.6 fusion.34
  107.4 0.2 copy.42
  107.6 1.1 convolution_convert_fusion.1
  108.7 0.2 all-gather.7.cloned.1.call-start
  108.9 0.5 all-gather.7.cloned.1.call-update
  109.4 0.1 copy.37
  109.8 4.5 reduce-window.6
  114.7 0.1 copy.36
  115.1 44.8 %all-gather.9.cloned.1.call-done = bf16[128,128,128]{2,1,0:T(8,128)(2,1)} async-done(((bf16[8,128,128]{2,1,0:T(8,128)(2,1)}), bf16[128,128,128]{2,1,0:T(8,128)(2,1)}) %all-gather.9.cloned.1.call-update) | async-done | bytes 4194320 | tf_op jit(solution)/shard_map/all_gather | solution.py:14
  159.9 20.1 %while.14 = (s32[]{:T(128)}, f32[8,128,128]{2,1,0:T(8,128)S(1)}, s32[]{:T(128)}, bf16[16,8,128,128]{3,2,1,0:T(8,128)(2,1)}, s32[]{:T(128)}, /*index=5*/s32[]{:T(128)}) while((s32[]{:T(128)}, f32[8,128,128]{2,1,0:T(8,128)S(1)}, s32[]{:T(128)}, bf16[16,8,128,128]{3,2,1,0:T(8,128)(2,1)}, s32[]{:T(128)}, /*index=5*/s32[]{:T(128)}) %tuple.44), condition=%wide.region_2.3_spmd.clone, body=%wide.region_1.2_spmd.clone.sunk | while | flops 524292 | bytes 1310813 | solution.py:22
  159.9 1.2 add_select_fusion.2
  161.2 1.2 add_select_fusion.2
  162.5 1.2 add_select_fusion.2
  163.7 1.2 add_select_fusion.2
  165.0 1.2 add_select_fusion.2
  166.2 1.2 add_select_fusion.2
  167.5 1.2 add_select_fusion.2
  168.7 1.2 add_select_fusion.2
  170.0 1.2 add_select_fusion.2
  171.3 1.2 add_select_fusion.2
  172.5 1.2 add_select_fusion.2
  173.8 1.3 add_select_fusion.2
  175.1 1.2 add_select_fusion.2
  176.3 1.2 add_select_fusion.2
  177.6 1.2 add_select_fusion.2
  178.9 1.2 add_select_fusion.2
  180.1 1.6 fusion.27
  181.7 2.0 multiply_reduce_fusion.1
  183.8 29.4 %all-gather.7.cloned.1.call-done = bf16[1024,2048]{1,0:T(8,128)(2,1)} async-done(((bf16[64,2048]{1,0:T(8,128)(2,1)}), bf16[1024,2048]{1,0:T(8,128)(2,1)}) %all-gather.7.cloned.1.call-update) | async-done | bytes 4194320 | tf_op jit(solution)/shard_map/all_gather | solution.py:79
  213.2 3.9 fusion.14
  217.1 0.2 fusion.15
  217.4 4.1 broadcast_in_dim.35
  221.5 6.9 %reshape.150 = bf16[1024,2048]{1,0:T(8,128)(2,1)} reshape(bf16[256,4,2048]{2,1,0:T(4,128)(2,1)} %broadcast_in_dim.35) | data formatting | bytes 8388608 | tf_op jit(solution)/shard_map/reshape | solution.py:89
  228.4 11.2 %scatter_custom_fusion = bf16[1536,2048]{1,0:T(8,128)(2,1)} fusion(s32[1024]{0:T(1024)S(1)} %bitcast.85, bf16[1024,2048]{1,0:T(8,128)(2,1)} %reshape.150, bf16[]{:T(256)} %constant.55.clone.1), kind=kCustom, calls=%fused_computation.12 | custom fusion | bytes 6291968 | tf_op jit(solution)/shard_map/scatter | solution.py:90
  239.6 77.4 %all_to_all.10 = bf16[16,96,2048]{2,1,0:T(8,128)(2,1)S(1)} all-to-all(bf16[16,96,2048]{2,1,0:T(8,128)(2,1)} %bitcast.77), channel_id=1, replica_groups=mesh['dp'=8,'ctx'=16] {'ctx'}, dimensions={0} | all-to-all | bytes 12582912 | tf_op jit(solution)/shard_map/all_to_all | solution.py:92
  317.1 16.2 %fusion.3 = f32[16,1,96,2048]{3,2,0,1:T(8,128)S(1)} fusion(bf16[16,96,2048]{2,1,0:T(8,128)(2,1)S(1)} %all_to_all.10, bf16[1,2048,2048]{2,1,0:T(8,128)(2,1)} %param.16), kind=kOutput, calls=%fused_computation.8 | convolution fusion | flops 12884901888 | bytes 27262976 | tf_op jit(solution)/shard_map/nxid,xdf->nxif/dot_general | solution.py:95
  333.3 8.6 %convolution_convert_fusion = bf16[16,96,2048]{2,1,0:T(8,128)(2,1)} fusion(bf16[1,1024,2048]{2,1,0:T(8,128)(2,1)S(1)} %copy-done.3, f32[16,1,96,2048]{3,2,0,1:T(8,128)S(1)} %fusion.3), kind=kOutput, calls=%fused_computation.9 | convolution fusion | flops 6455033856 | bytes 23068672 | tf_op jit(solution)/shard_map/nxif,xfd->nxid/dot_general | solution.py:97
  341.9 8.0 %all-to-all-start.1 = ((bf16[16,96,2048]{2,1,0:T(8,128)(2,1)}), bf16[16,96,2048]{2,1,0:T(8,128)(2,1)}, u32[]{:S(2)}, u32[]{:S(2)}) async-start(bf16[16,96,2048]{2,1,0:T(8,128)(2,1)} %convolution_convert_fusion), calls=%async_computation.1 | async-start | bytes 12582912 | tf_op jit(solution)/shard_map/all_to_all | solution.py:101
  349.9 0.1 copy.35
  350.1 92.1 %all-to-all-done.1 = bf16[16,96,2048]{2,1,0:T(8,128)(2,1)} async-done(((bf16[16,96,2048]{2,1,0:T(8,128)(2,1)}), bf16[16,96,2048]{2,1,0:T(8,128)(2,1)}, u32[]{:S(2)}, u32[]{:S(2)}) %all-to-all-start.1) | async-done | bytes 6291488 | tf_op jit(solution)/shard_map/all_to_all | solution.py:101
  442.2 12.4 %gather_fusion = bf16[1024,2048]{1,0:T(8,128)(2,1)} fusion(bf16[1536,2048]{1,0:T(8,128)(2,1)} %bitcast.18, s32[1024]{0:T(1024)S(1)} %broadcast_clamp_fusion), kind=kCustom, calls=%fused_computation | custom fusion | bytes 8392704 | tf_op jit(solution)/shard_map/gather | solution.py:104
  454.6 8.3 %reshape.137 = f32[256,4,2048]{2,1,0:T(4,128)} reshape(bf16[1024,2048]{1,0:T(8,128)(2,1)} %gather_fusion) | data formatting | bytes 12582912 | tf_op jit(solution)/shard_map/convert_element_type | solution.py:104
  462.9 10.0 %multiply_reduce_fusion = f32[256,2048]{1,0:T(8,128)S(1)} fusion(f32[256,4,2048]{2,1,0:T(4,128)} %reshape.137, f32[256,4]{1,0:T(8,128)S(1)} %copy.35), kind=kLoop, calls=%fused_computation.5 | loop fusion | flops 3670016 | bytes 10489856 | tf_op jit(solution)/shard_map/reduce_sum | solution.py:105
  472.9 1.3 fusion.16
  (32 shorter events, 1.1 us)
Async XLA Ops:
  6.5 93.4 %all-gather.5.cloned.1.call-start = ((), (), s32[]{:S(2)}) async-start(), calls=%async_computation.2 | async-start | bytes 13369344 | tf_op jit(solution)/shard_map/all_gather | solution.py:48
  7.3 152.7 %all-gather.9.cloned.1.call-start = ((), (), s32[]{:S(2)}) async-start(), calls=%async_computation.4 | async-start | bytes 4456448 | tf_op jit(solution)/shard_map/all_gather | solution.py:14
  106.7 2.7 copy-start.1
  108.7 71.4 %copy-start = (f32[8,128,128]{2,1,0:T(8,128)S(1)}, f32[8,128,128]{2,1,0:T(8,128)}, u32[]{:S(2)}) copy-start(f32[8,128,128]{2,1,0:T(8,128)} %param.13) | copy-start | bytes 1572868
  108.7 104.5 %all-gather.7.cloned.1.call-start = ((), (), s32[]{:S(2)}) async-start(), calls=%async_computation.3 | async-start | bytes 4456448 | tf_op jit(solution)/shard_map/all_gather | solution.py:79
  317.1 16.2 %copy-start.3 = (bf16[1,1024,2048]{2,1,0:T(8,128)(2,1)S(1)}, bf16[1,1024,2048]{2,1,0:T(8,128)(2,1)}, u32[]{:S(2)}) copy-start(bf16[1,1024,2048]{2,1,0:T(8,128)(2,1)} %param.17) | copy-start | bytes 12582916
  341.9 8.0 %copy-start.2 = (f32[256,4]{0,1:T(4,128)S(1)}, f32[256,4]{0,1:T(4,128)}, u32[]{:S(2)}) copy-start(f32[256,4]{0,1:T(4,128)} %param.15) | copy-start | bytes 12292
  341.9 100.3 %all-to-all-start.1 = ((bf16[16,96,2048]{2,1,0:T(8,128)(2,1)}), bf16[16,96,2048]{2,1,0:T(8,128)(2,1)}, u32[]{:S(2)}, u32[]{:S(2)}) async-start(bf16[16,96,2048]{2,1,0:T(8,128)(2,1)} %convolution_convert_fusion), calls=%async_computation.1 | async-start | bytes 12582912 | tf_op jit(solution)/shard_map/all_to_all | solution.py:101
Sparse Core Ops, SparseCore 0:
  9.5 90.3 all-gather.4
  108.8 51.0 all-gather.8
  162.1 51.0 all-gather.6
where the time goes:
time: 482 us; the launch traced here: 481 us
  waiting for transfers between devices  259 us (54%)
  blocking collectives  77.4 us (16%)
  local copies, waits for them, and re-layouts  44.3 us (9%)
  matrix products  40.1 us (8%)
  other arithmetic  38.2 us (8%)
  between operations  13.3 us (3%)
  starting transfers between devices  8.26 us (2%)
    all_to_all x1, waiting for transfers between devices, shards(): lax.all_to_all(finished, 'ctx', split_axis=0, concat_axis=0, tiled=True)  92.1 us
    all_gather x1, waiting for transfers between devices, shards(): lax.all_gather(qkv_weight, 'ctx', axis=0, tiled=True)  91.1 us
    all_to_all x1, blocking collectives, shards(): lax.all_to_all(outgoing, 'ctx', split_axis=0, concat_axis=0, tiled=True)  77.4 us
    all_gather x1, waiting for transfers between devices, prefix(): everything = lax.all_gather(x.astype(jnp.bfloat16), axis)  44.8 us
    all_gather x1, waiting for transfers between devices, shards(): lax.all_gather(out_weight, 'ctx', axis=0, tiled=True)  29.4 us
    select_n x16, other arithmetic, step(): return jnp.where(reached, new, before)  19.8 us
    dot_general x1, matrix products, shards(): jnp.einsum('nxid,xdf->nxif', grouped, expert_in, preferred_element_type=j...  16.2 us
    gather x1, local copies, waits for them, and re-layouts, shards(): returned[places].reshape(tok_rows, top_count, model_width)  12.4 us
  transfers between devices with their start and end apart: 4, of which 4 were waited for; matrix products, arithmetic and copies ran while one was open for 6% of the time, Pallas kernels for 0%

commit v1 on v0

--- a/solution.py
+++ b/solution.py
@@ -76,7 +76,9 @@
     columns = head_normed
     attended = jnp.dot(
         columns,
-        lax.all_gather(out_weight, "ctx", axis=0, tiled=True),
+        jnp.concatenate(
+            lax.all_to_all(jnp.stack([out_weight] * lax.axis_size("ctx")), "ctx", 0, 0), axis=0
+        ),
         preferred_element_type=jnp.float32,
     )
     hidden = (tokens.astype(jnp.float32) + attended).astype(jnp.bfloat16)

time: 482 us -> 498 us (1.033)
  starting transfers between devices: 8.26 us -> 15.4 us
  waiting for transfers between devices: 259 us -> 265 us
    all_gather x1, waiting for transfers between devices: 44.8 us -> 80.9 us  [prefix(): everything = lax.all_gather(x.astype(jnp.bfloat16), axis)]
    all_gather x1 -> x0, waiting for transfers between devices: 29.4 us -> none  [shards(): lax.all_gather(out_weight, 'ctx', axis=0, tiled=True)]
    all_to_all x0 -> x1, starting transfers between devices: none -> 7.36 us  [shards(): lax.all_to_all(jnp.stack([out_weight] * lax.axis_size('ctx')), 'ctx', 0, 0)]
  transfers between devices with their start and end apart: 4 -> 4, of which waited for: 4 -> 3; matrix products, arithmetic and copies ran while one was open for 6% -> 7% of each run, Pallas kernels for 0% -> 0%
where the time goes in v1:
time: 498 us; the launch traced here: 497 us
  waiting for transfers between devices  265 us (53%)
  blocking collectives  77.4 us (16%)
  local copies, waits for them, and re-layouts  46.8 us (9%)
  matrix products  40.1 us (8%)
  other arithmetic  38.2 us (8%)
  starting transfers between devices  15.4 us (3%)
  between operations  13.6 us (3%)
    all_to_all x1, waiting for transfers between devices, shards(): lax.all_to_all(finished, 'ctx', split_axis=0, concat_axis=0, tiled=True)  92.2 us
    all_gather x1, waiting for transfers between devices, shards(): lax.all_gather(qkv_weight, 'ctx', axis=0, tiled=True)  91.1 us
    all_gather x1, waiting for transfers between devices, prefix(): everything = lax.all_gather(x.astype(jnp.bfloat16), axis)  80.9 us
    all_to_all x1, blocking collectives, shards(): lax.all_to_all(outgoing, 'ctx', split_axis=0, concat_axis=0, tiled=True)  77.4 us
    select_n x16, other arithmetic, step(): return jnp.where(reached, new, before)  19.8 us
    dot_general x1, matrix products, shards(): jnp.einsum('nxid,xdf->nxif', grouped, expert_in, preferred_element_type=j...  16.2 us
    gather x1, local copies, waits for them, and re-layouts, shards(): returned[places].reshape(tok_rows, top_count, model_width)  12.4 us
    scatter x1, local copies, waits for them, and re-layouts, shards(): jnp.zeros((experts * capacity, model_width), jnp.bfloat16).at[places]  11.2 us
  transfers between devices with their start and end apart: 4, of which 3 were waited for; matrix products, arithmetic and copies ran while one was open for 7% of the time, Pallas kernels for 0%

profile of v1, /device:TPU:28, one launch (start us, length us, event | category | flops | bytes accessed | tf_op | source)
XLA Modules:
  0.0 496.8 jit_solution(14243297754956165089)
XLA Ops:
  6.5 0.7 all-gather.4.cloned.1.call-update
  7.3 1.5 fusion.12
  8.8 91.1 %all-gather.4.cloned.1.call-done = bf16[2048,3072]{1,0:T(8,128)(2,1)} async-done(((bf16[128,3072]{1,0:T(8,128)(2,1)}), bf16[2048,3072]{1,0:T(8,128)(2,1)}) %all-gather.4.cloned.1.call-update) | async-done | bytes 12582928 | tf_op jit(solution)/shard_map/all_gather | solution.py:48
  99.9 6.8 %fusion.20 = f32[256,3072]{1,0:T(8,128)S(1)} fusion(bf16[2048,3072]{1,0:T(8,128)(2,1)} %all-gather.4.cloned.1.call-done, bf16[256,2048]{1,0:T(8,128)(2,1)} %param.10, f32[256]{0:T(256)S(1)} %add_rsqrt_fusion.2), kind=kOutput, calls=%fused_computation.31 | convolution fusion | flops 3222798336 | bytes 16778240 | tf_op jit(solution)/shard_map/dot_general | solution.py:46
  106.7 0.6 fusion.34
  107.4 0.2 copy.42
  107.6 1.1 convolution_convert_fusion.1
  108.7 2.5 stack.2
  111.2 7.4 %all-to-all-start = ((bf16[16,64,2048]{2,1,0:T(8,128)(2,1)}), bf16[16,64,2048]{2,1,0:T(8,128)(2,1)}, u32[]{:S(2)}, u32[]{:S(2)}) async-start(bf16[16,64,2048]{2,1,0:T(8,128)(2,1)} %stack.2), calls=%async_computation | async-start | bytes 8388608 | tf_op jit(solution)/shard_map/all_to_all | solution.py:80
  118.6 0.1 copy.37
  119.0 4.5 reduce-window.6
  123.6 0.1 copy.39
  123.8 0.1 copy.36
  124.3 80.9 %all-gather.6.cloned.1.call-done = bf16[128,128,128]{2,1,0:T(8,128)(2,1)} async-done(((bf16[8,128,128]{2,1,0:T(8,128)(2,1)}), bf16[128,128,128]{2,1,0:T(8,128)(2,1)}) %all-gather.6.cloned.1.call-update) | async-done | bytes 4194320 | tf_op jit(solution)/shard_map/all_gather | solution.py:14
  205.1 20.1 %while.14 = (s32[]{:T(128)}, f32[8,128,128]{2,1,0:T(8,128)S(1)}, s32[]{:T(128)}, bf16[16,8,128,128]{3,2,1,0:T(8,128)(2,1)}, s32[]{:T(128)}, /*index=5*/s32[]{:T(128)}) while((s32[]{:T(128)}, f32[8,128,128]{2,1,0:T(8,128)S(1)}, s32[]{:T(128)}, bf16[16,8,128,128]{3,2,1,0:T(8,128)(2,1)}, s32[]{:T(128)}, /*index=5*/s32[]{:T(128)}) %tuple.42), condition=%wide.region_2.3_spmd.clone, body=%wide.region_1.2_spmd.clone.sunk | while | flops 524292 | bytes 1310813 | solution.py:22
  205.2 1.2 add_select_fusion.2
  206.4 1.2 add_select_fusion.2
  207.7 1.2 add_select_fusion.2
  208.9 1.2 add_select_fusion.2
  210.2 1.2 add_select_fusion.2
  211.4 1.2 add_select_fusion.2
  212.7 1.2 add_select_fusion.2
  214.0 1.2 add_select_fusion.2
  215.2 1.2 add_select_fusion.2
  216.5 1.2 add_select_fusion.2
  217.7 1.2 add_select_fusion.2
  219.0 1.2 add_select_fusion.2
  220.2 1.2 add_select_fusion.2
  221.5 1.2 add_select_fusion.2
  222.8 1.2 add_select_fusion.2
  224.0 1.2 add_select_fusion.2
  225.3 1.6 fusion.27
  226.9 2.0 multiply_reduce_fusion.1
  229.0 3.9 fusion.14
  232.9 0.2 fusion.15
  233.1 4.1 broadcast_in_dim.35
  237.2 6.9 %reshape.156 = bf16[1024,2048]{1,0:T(8,128)(2,1)} reshape(bf16[256,4,2048]{2,1,0:T(4,128)(2,1)} %broadcast_in_dim.35) | data formatting | bytes 8388608 | tf_op jit(solution)/shard_map/reshape | solution.py:91
  244.1 11.2 %scatter_custom_fusion = bf16[1536,2048]{1,0:T(8,128)(2,1)} fusion(s32[1024]{0:T(1024)S(1)} %bitcast.86, bf16[1024,2048]{1,0:T(8,128)(2,1)} %reshape.156, bf16[]{:T(256)} %constant.55.clone.1), kind=kCustom, calls=%fused_computation.12 | custom fusion | bytes 6291968 | tf_op jit(solution)/shard_map/scatter | solution.py:92
  255.4 77.4 %all_to_all.15 = bf16[16,96,2048]{2,1,0:T(8,128)(2,1)S(1)} all-to-all(bf16[16,96,2048]{2,1,0:T(8,128)(2,1)} %bitcast.78), channel_id=1, replica_groups=mesh['dp'=8,'ctx'=16] {'ctx'}, dimensions={0} | all-to-all | bytes 12582912 | tf_op jit(solution)/shard_map/all_to_all | solution.py:94
  332.8 16.2 %fusion.3 = f32[16,1,96,2048]{3,2,0,1:T(8,128)S(1)} fusion(bf16[16,96,2048]{2,1,0:T(8,128)(2,1)S(1)} %all_to_all.15, bf16[1,2048,2048]{2,1,0:T(8,128)(2,1)} %param.16), kind=kOutput, calls=%fused_computation.8 | convolution fusion | flops 12884901888 | bytes 27262976 | tf_op jit(solution)/shard_map/nxid,xdf->nxif/dot_general | solution.py:97
  349.0 8.6 %convolution_convert_fusion = bf16[16,96,2048]{2,1,0:T(8,128)(2,1)} fusion(bf16[1,1024,2048]{2,1,0:T(8,128)(2,1)S(1)} %copy-done.4, f32[16,1,96,2048]{3,2,0,1:T(8,128)S(1)} %fusion.3), kind=kOutput, calls=%fused_computation.9 | convolution fusion | flops 6455033856 | bytes 23068672 | tf_op jit(solution)/shard_map/nxif,xfd->nxid/dot_general | solution.py:99
  357.6 8.0 %all-to-all-start.2 = ((bf16[16,96,2048]{2,1,0:T(8,128)(2,1)}), bf16[16,96,2048]{2,1,0:T(8,128)(2,1)}, u32[]{:S(2)}, u32[]{:S(2)}) async-start(bf16[16,96,2048]{2,1,0:T(8,128)(2,1)} %convolution_convert_fusion), calls=%async_computation.2 | async-start | bytes 12582912 | tf_op jit(solution)/shard_map/all_to_all | solution.py:103
  365.6 0.1 copy.35
  365.8 92.2 %all-to-all-done.2 = bf16[16,96,2048]{2,1,0:T(8,128)(2,1)} async-done(((bf16[16,96,2048]{2,1,0:T(8,128)(2,1)}), bf16[16,96,2048]{2,1,0:T(8,128)(2,1)}, u32[]{:S(2)}, u32[]{:S(2)}) %all-to-all-start.2) | async-done | bytes 6291488 | tf_op jit(solution)/shard_map/all_to_all | solution.py:103
  458.0 12.4 %gather_fusion = bf16[1024,2048]{1,0:T(8,128)(2,1)} fusion(bf16[1536,2048]{1,0:T(8,128)(2,1)} %bitcast.19, s32[1024]{0:T(1024)S(1)} %broadcast_clamp_fusion), kind=kCustom, calls=%fused_computation | custom fusion | bytes 8392704 | tf_op jit(solution)/shard_map/gather | solution.py:106
  470.4 8.3 %reshape.143 = f32[256,4,2048]{2,1,0:T(4,128)} reshape(bf16[1024,2048]{1,0:T(8,128)(2,1)} %gather_fusion) | data formatting | bytes 12582912 | tf_op jit(solution)/shard_map/convert_element_type | solution.py:106
  478.7 10.0 %multiply_reduce_fusion = f32[256,2048]{1,0:T(8,128)S(1)} fusion(f32[256,4,2048]{2,1,0:T(4,128)} %reshape.143, f32[256,4]{1,0:T(8,128)S(1)} %copy.35), kind=kLoop, calls=%fused_computation.5 | loop fusion | flops 3670016 | bytes 10489856 | tf_op jit(solution)/shard_map/reduce_sum | solution.py:107
  488.7 1.3 fusion.16
  (34 shorter events, 1.0 us)
Async XLA Ops:
  6.5 93.4 %all-gather.4.cloned.1.call-start = ((), (), s32[]{:S(2)}) async-start(), calls=%async_computation.3 | async-start | bytes 13369344 | tf_op jit(solution)/shard_map/all_gather | solution.py:48
  7.3 197.9 %all-gather.6.cloned.1.call-start = ((), (), s32[]{:S(2)}) async-start(), calls=%async_computation.4 | async-start | bytes 4456448 | tf_op jit(solution)/shard_map/all_gather | solution.py:14
  106.7 1.9 copy-start.1
  111.2 7.4 %copy-start.2 = (s32[256,4]{0,1:T(4,128)S(1)}, s32[256,4]{0,1:T(4,128)}, u32[]{:S(2)}) copy-start(s32[256,4]{0,1:T(4,128)} %param.14) | copy-start | bytes 12292
  111.2 117.8 %all-to-all-start = ((bf16[16,64,2048]{2,1,0:T(8,128)(2,1)}), bf16[16,64,2048]{2,1,0:T(8,128)(2,1)}, u32[]{:S(2)}, u32[]{:S(2)}) async-start(bf16[16,64,2048]{2,1,0:T(8,128)(2,1)} %stack.2), calls=%async_computation | async-start | bytes 8388608 | tf_op jit(solution)/shard_map/all_to_all | solution.py:80
  118.5 106.7 %copy-start = (f32[8,128,128]{2,1,0:T(8,128)S(1)}, f32[8,128,128]{2,1,0:T(8,128)}, u32[]{:S(2)}) copy-start(f32[8,128,128]{2,1,0:T(8,128)} %param.13) | copy-start | bytes 1572868
  332.8 16.2 %copy-start.4 = (bf16[1,1024,2048]{2,1,0:T(8,128)(2,1)S(1)}, bf16[1,1024,2048]{2,1,0:T(8,128)(2,1)}, u32[]{:S(2)}) copy-start(bf16[1,1024,2048]{2,1,0:T(8,128)(2,1)} %param.17) | copy-start | bytes 12582916
  357.6 8.0 %copy-start.3 = (f32[256,4]{0,1:T(4,128)S(1)}, f32[256,4]{0,1:T(4,128)}, u32[]{:S(2)}) copy-start(f32[256,4]{0,1:T(4,128)} %param.15) | copy-start | bytes 12292
  357.6 100.3 %all-to-all-start.2 = ((bf16[16,96,2048]{2,1,0:T(8,128)(2,1)}), bf16[16,96,2048]{2,1,0:T(8,128)(2,1)}, u32[]{:S(2)}, u32[]{:S(2)}) async-start(bf16[16,96,2048]{2,1,0:T(8,128)(2,1)} %convolution_convert_fusion), calls=%async_computation.2 | async-start | bytes 12582912 | tf_op jit(solution)/shard_map/all_to_all | solution.py:103
Sparse Core Ops, SparseCore 0:
  9.5 90.3 all-gather.3
  108.8 96.3 all-gather.5
